TPU v7x, 128 devices: a whole 4x4x4 slice. The times are simulated.
128 devices in a mesh: ctx: 32 (over y, z, core), exp: 4 (over x).
Axes of the slice: x: 4, y: 4, z: 4, core: 2. Of those that a mesh axis runs over, the one named last changes fastest.
Arguments:
- inputs: bfloat16 [4096, 4096], P('ctx', 'exp'), may hold values from -6 to 6
- gate_input: bfloat16 [4096, 4096], P('ctx', 'exp')
- b_proj: bfloat16 [4096, 128], P('ctx'), may hold values from -0.5 to 0.5
- c_proj: bfloat16 [4096, 128], P('ctx'), may hold values from -6 to 6
- step_size: float32 [64, 4096], P('exp', 'ctx'), may hold values from 0.03 to 0.3
- decay_rate: float32 [64, 4096], P('exp', 'ctx'), as said below
- skip_gain: float32 [64], P('exp'), may hold values from 0.5 to 2
- start_state: float32 [64, 64, 128], P('exp'), may hold values from -3 to 3
- norm_gain: float32 [4096], P('exp'), may hold values from 0.5 to 1.5
- out_proj: bfloat16 [4096, 4096], P('exp', 'ctx'), may hold values from -0.09375 to 0.09375
- residual: bfloat16 [4096, 4096], P('ctx'), may hold values from -6 to 6
- moe_gain: float32 [4096], replicated, may hold values from 0.5 to 1.5
- w_gate: bfloat16 [32, 4096, 3584], P('ctx', None, 'exp'), may hold values from -0.09375 to 0.09375
- w_up: bfloat16 [32, 4096, 3584], P('ctx', None, 'exp'), may hold values from -0.09375 to 0.09375
- w_down: bfloat16 [32, 3584, 4096], P('ctx', 'exp'), may hold values from -0.0625 to 0.0625
- route_ids: int32 [4096, 2], P('ctx'), may hold values from 0 to 15, all different within a row; in each aligned block of 32 rows (0 to 31, 32 to 63, ...) at most 8 rows name the same one
- route_gates: float32 [4096, 2], P('ctx'), may hold values from 0.3 to 1
Outputs:
- output: bfloat16 [4096, 4096], P(('ctx', 'exp'))
Inputs may be any that keep to these rules, and one draw needn't show every extreme that they name: `route_ids`: each row names two different experts. In each aligned block of 32 rows no expert is named more than 8 times, a bound that some block reaches. `decay_rate`: Non-negative.
All inputs are finite; a program needn't handle non-finite values.
Results may differ from a plain program's by a relative error of at most 0.02.
Values may be sent and summed in bfloat16 or wider, within the bound.
A program may use at most 128 MiB of HBM per device.

v0:
```python
import jax
import jax.numpy as jnp
from jax import lax
from jax.sharding import PartitionSpec as P

PAIR = 2
eps_norm = 1e-05
top_precision = lax.Precision.HIGHEST


def entering(x, axis, join, neutral):
    place = lax.axis_index(axis)
    gathered = jax.tree.map(
        lambda a, kind: lax.all_gather(a.astype(kind), axis), x, (jnp.bfloat16, jnp.bfloat16)
    )
    state = jax.tree.map(lambda a, e: jnp.zeros_like(a) + jnp.asarray(e, a.dtype), x, neutral)

    def one(hop, state):
        return join(
            state,
            jax.tree.map(
                lambda a, own: lax.dynamic_index_in_dim(a, hop, 0, False).astype(own.dtype),
                gathered,
                x,
            ),
        )

    return lax.fori_loop(0, place, one, state)


def later_state(earlier, later):
    first_decay, first_state = earlier
    second_decay, second_state = later
    return (first_decay * second_decay, second_decay[:, None, None] * first_state + second_state)


def route_ranks(quarter_ids, experts):
    flattened = quarter_ids.reshape(-1)
    onehot = (flattened[:, None] == jnp.arange(experts, dtype=jnp.int32)[None, :]).astype(jnp.int32)
    running = jnp.cumsum(onehot, axis=0)
    rank_ids = jnp.sum(onehot * running, axis=1) - 1
    return (flattened, rank_ids)


def place_rows(normed, quarter_ids, experts, capacity):
    flattened, rank_ids = route_ranks(quarter_ids, experts)
    slot_ids = rank_ids * experts + flattened
    matches = (
        jnp.arange(capacity * experts, dtype=jnp.int32)[:, None] == slot_ids[None, :]
    ).astype(jnp.bfloat16)
    doubled = jnp.repeat(normed, quarter_ids.shape[1], axis=0)
    placed = jnp.dot(matches, doubled, preferred_element_type=jnp.float32).astype(jnp.bfloat16)
    return placed.reshape(capacity, experts, normed.shape[1])


def rms_rows(values, gain_vec):
    scaling = lax.rsqrt(jnp.mean(values * values, axis=1, keepdims=True) + eps_norm)
    return (values * scaling * gain_vec[None, :]).astype(jnp.bfloat16)


def local(
    inputs,
    gate_input,
    b_proj,
    c_proj,
    step_size,
    decay_rate,
    skip_gain,
    start_state,
    norm_gain,
    out_proj,
    residual,
    moe_gain,
    w_gate,
    w_up,
    w_down,
    route_ids,
    route_gates,
):
    tok_ctx = inputs.shape[0]
    head_count = step_size.shape[0]
    head_dim = inputs.shape[1] // head_count
    model_width = residual.shape[1]
    n_ctx = lax.axis_size("ctx")
    n_exp = lax.axis_size("exp")
    experts = n_ctx // PAIR
    tok_quarter = tok_ctx // n_exp
    capacity = 4 * tok_quarter // experts
    x_local = inputs.astype(jnp.float32).reshape(tok_ctx, head_count, head_dim)
    b_local = b_proj.astype(jnp.float32)
    c_local = c_proj.astype(jnp.float32)
    cumulative = jnp.cumsum(decay_rate, axis=1)
    span_total = cumulative[:, -1]
    sequence_indices = jnp.arange(tok_ctx, dtype=jnp.int32)
    causal = sequence_indices[:, None] >= sequence_indices[None, :]
    spread = jnp.where(causal[None], cumulative[:, :, None] - cumulative[:, None, :], 0.0)
    scores = jnp.dot(c_local, b_local.T, precision=top_precision)
    mixing = jnp.where(causal[None], jnp.exp(-spread), 0.0) * scores[None] * step_size[:, None, :]
    inside_part = jnp.einsum("hts,shp->thp", mixing, x_local, precision=top_precision)
    ending = jnp.exp(-(span_total[:, None] - cumulative)) * step_size
    local_state = jnp.einsum("hs,shp,sn->hpn", ending, x_local, b_local, precision=top_precision)
    prior_decay, prior_state = entering(
        (jnp.exp(-span_total), local_state),
        "ctx",
        later_state,
        (jnp.ones_like(span_total), jnp.zeros_like(local_state)),
    )
    incoming = prior_state + prior_decay[:, None, None] * start_state
    carried = (
        jnp.einsum("hpn,tn->thp", incoming, c_local, precision=top_precision)
        * jnp.exp(-cumulative).T[:, :, None]
    )
    ssm_out = inside_part + carried + skip_gain[None, :, None] * x_local
    gated_out = ssm_out.reshape(tok_ctx, head_count * head_dim) * jax.nn.silu(
        gate_input.astype(jnp.float32)
    )
    squares = lax.psum(jnp.sum(gated_out * gated_out, axis=1), "exp")
    scaling = lax.rsqrt(squares / (head_count * head_dim * n_exp) + eps_norm)
    normed_mix = (gated_out * scaling[:, None] * norm_gain[None, :]).astype(jnp.bfloat16)
    partial_value = jnp.dot(
        normed_mix,
        lax.all_gather(out_proj, "ctx", axis=1, tiled=True),
        preferred_element_type=jnp.float32,
    )
    gate_rows = w_gate[0]
    up_rows = w_up[0]
    down_rows = w_down[0]
    piece_width = gate_rows.shape[1]
    first_row = lax.axis_index("exp") * tok_quarter
    own_ids = lax.dynamic_slice_in_dim(route_ids, first_row, tok_quarter, 0)
    own_gates = lax.dynamic_slice_in_dim(route_gates, first_row, tok_quarter, 0)
    mixed_all = lax.psum(partial_value.astype(jnp.bfloat16), "exp").astype(jnp.float32)
    hidden_all = residual.astype(jnp.float32) + mixed_all
    moe_all = rms_rows(hidden_all, moe_gain)

    def place_quarter(quarter_rows, quarter_ids):
        return place_rows(quarter_rows, quarter_ids, experts, capacity)

    placed = jax.vmap(place_quarter)(
        moe_all.reshape(n_exp, tok_quarter, model_width),
        route_ids.reshape(n_exp, tok_quarter, route_ids.shape[1]),
    )
    placed = placed.reshape(n_exp * capacity, experts, model_width)
    outgoing = jnp.repeat(placed, PAIR, axis=1)
    arrived = lax.all_to_all(outgoing, "ctx", split_axis=1, concat_axis=1, tiled=True)
    flattened = arrived.reshape(-1, model_width)
    gate_val = jnp.dot(flattened, gate_rows, preferred_element_type=jnp.float32)
    up_val = jnp.dot(flattened, up_rows, preferred_element_type=jnp.float32)
    activated = (jax.nn.silu(gate_val) * up_val).astype(jnp.bfloat16)
    hidden = activated.reshape(arrived.shape[0], arrived.shape[1], piece_width)
    hidden_own = lax.dynamic_slice_in_dim(hidden_all, first_row, tok_quarter, 0)
    product = jnp.dot(
        hidden.reshape(-1, piece_width), down_rows, preferred_element_type=jnp.float32
    )
    rounded = lax.optimization_barrier(product.astype(jnp.bfloat16)).astype(jnp.float32)
    summed = lax.psum_scatter(
        rounded.reshape(lax.axis_size("exp") * capacity, hidden.shape[1], model_width).astype(
            jnp.bfloat16
        ),
        "exp",
        scatter_dimension=0,
        tiled=True,
    )
    halves = lax.all_to_all(summed, "ctx", split_axis=1, concat_axis=1, tiled=True)
    flattened, rank_ids = route_ranks(own_ids, experts)
    base_rows = rank_ids * n_ctx + flattened * PAIR
    fetch_rows = base_rows[:, None] + jnp.arange(PAIR, dtype=jnp.int32)[None, :]
    fetched = halves.reshape(capacity * n_ctx, model_width)[fetch_rows]
    expert_out = jnp.sum(fetched.astype(jnp.float32), axis=1)
    weighted = expert_out * own_gates.reshape(-1)[:, None]
    moe_out = jnp.sum(weighted.reshape(tok_quarter, -1, model_width), axis=1)
    return (hidden_own + moe_out).astype(jnp.bfloat16)


def solution(mesh):
    in_specs = (
        P("ctx", "exp"),
        P("ctx", "exp"),
        P("ctx", None),
        P("ctx", None),
        P("exp", "ctx"),
        P("exp", "ctx"),
        P("exp"),
        P("exp", None, None),
        P("exp"),
        P("exp", "ctx"),
        P("ctx", None),
        P(),
        P("ctx", None, "exp"),
        P("ctx", None, "exp"),
        P("ctx", "exp", None),
        P("ctx", None),
        P("ctx", None),
    )
    out_specs = P(("ctx", "exp"), None)
    return jax.shard_map(local, mesh=mesh, in_specs=in_specs, out_specs=out_specs, check_vma=False)
```

profile of v0, /device:TPU:1, one launch (start us, length us, event | category | flops | bytes accessed | tf_op | source)
XLA Modules:
  0.0 490.3 jit_solution(6920894452097007620)
XLA Ops:
  7.7 1.1 copy.61
  9.6 1.1 convolution_convert_fusion.3
  11.6 1.2 dynamic-slice
  13.8 65.5 %all-reduce = bf16[512]{0:T(512)(128)(2,1)S(1)} all-reduce(bf16[512]{0:T(512)(128)(2,1)S(1)} %dynamic-update-slice), channel_id=2, replica_groups=mesh['ctx'=32,'exp'=4] {'ctx'}, use_global_device_ids=true, to_apply=%add | all-reduce | flops 512 | bytes 2048
  80.5 1.2 while.12
  80.5 1.1 convert_add_fusion.3
  82.2 1.4 fusion.8
  84.1 8.4 %psum.14 = f32[128]{0:T(128)S(1)} all-reduce(f32[128]{0:T(128)S(1)} %multiply_reduce_fusion.2), channel_id=1, replica_groups=mesh['ctx'=32,'exp'=4] {'exp'}, use_global_device_ids=true, to_apply=%region_4.5 | all-reduce | flops 128 | bytes 1024 | tf_op jit(solution)/shard_map/psum | solution.py:117
  92.5 36.7 %all-gather.5.cloned.1.call-done = bf16[1024,4096]{1,0:T(8,128)(2,1)} async-done(((bf16[1024,128]{1,0:T(8,128)(2,1)}), bf16[1024,4096]{1,0:T(8,128)(2,1)}) %all-gather.5.cloned.1.call-update) | async-done | bytes 8388624 | tf_op jit(solution)/shard_map/all_gather | solution.py:122
  129.2 5.8 %convolution_convert_fusion.2 = bf16[128,4096]{1,0:T(8,128)(2,1)} fusion(bf16[1024,4096]{1,0:T(8,128)(2,1)} %all-gather.5.cloned.1.call-done, f32[1024]{0:T(1024)S(1)} %copy-done.12, f32[128]{0:T(128)S(1)} %add_rsqrt_fusion.1, f32[128,1024]{1,0:T(8,128)S(1)} %copy.62, bf16[128,1024]{1,0:T(8,128)(2,1)S(1)} %copy-done.6), kind=kOutput, calls=%fused_computation.10 | convolution fusion | flops 1075445760 | bytes 10228224 | tf_op jit(solution)/shard_map/dot_general | solution.py:120
  135.8 42.9 %all-reduce.3.cloned.1.call-done = bf16[128,4096]{1,0:T(8,128)(2,1)} async-done(((bf16[128,4096]{1,0:T(8,128)(2,1)}), bf16[128,4096]{1,0:T(8,128)(2,1)}) %all-reduce.3.cloned.1.call-update) | async-done | bytes 1048592 | tf_op jit(solution)/shard_map/psum | solution.py:132
  178.8 3.0 convert_add_fusion.1
  182.2 3.4 broadcast_in_dim.28
  185.7 2.7 reshape.157
  188.4 1.4 convolution_convert_fusion.1
  189.8 2.3 copy.64
  192.1 4.3 broadcast_in_dim.29
  196.3 105.0 %all_to_all.10 = bf16[32,32,4096]{2,0,1:T(8,128)(2,1)} all-to-all(bf16[32,32,4096]{2,0,1:T(8,128)(2,1)} %bitcast.66), channel_id=1, replica_groups=mesh['ctx'=32,'exp'=4] {'ctx'}, dimensions={1} | all-to-all | bytes 16777216 | tf_op jit(solution)/shard_map/all_to_all | solution.py:145
  301.4 11.3 %copy.65 = bf16[32,32,4096]{2,1,0:T(8,128)(2,1)} copy(bf16[32,32,4096]{2,0,1:T(8,128)(2,1)} %all_to_all.10) | data formatting | bytes 16777216 | tf_op jit(solution)/shard_map/all_to_all | solution.py:145
  312.7 13.0 %fusion.1 = f32[1024,896]{1,0:T(8,128)S(1)} fusion(bf16[1024,4096]{1,0:T(8,128)(2,1)} %bitcast.68, bf16[1,4096,896]{2,1,0:T(8,128)(2,1)} %param.32), kind=kOutput, calls=%fused_computation.5 | convolution fusion | flops 7516192768 | bytes 19398656 | tf_op jit(solution)/shard_map/dot_general | solution.py:148
  325.8 9.2 %multiply_convert_fusion = bf16[1024,896]{1,0:T(8,128)(2,1)S(1)} fusion(f32[1024,896]{1,0:T(8,128)S(1)} %fusion.1, bf16[1024,4096]{1,0:T(8,128)(2,1)S(1)} %bitcast.69, bf16[1,4096,896]{2,1,0:T(8,128)(2,1)S(1)} %bitcast.78), kind=kOutput, calls=%fused_computation.11 | convolution fusion | flops 7521697792 | bytes 21233664 | tf_op jit(solution)/shard_map/dot_general | solution.py:147
  335.0 11.2 %convolution_convert_fusion = bf16[1024,4096]{1,0:T(8,128)(2,1)} fusion(bf16[1024,896]{1,0:T(8,128)(2,1)S(1)} %multiply_convert_fusion, bf16[1,896,4096]{2,1,0:T(8,128)(2,1)S(1)} %bitcast.80), kind=kOutput, calls=%fused_computation.3 | convolution fusion | flops 7520387072 | bytes 17563648 | tf_op jit(solution)/shard_map/dot_general | solution.py:152
  346.2 11.3 %copy.74 = bf16[4,8,32,4096]{3,1,2,0:T(8,128)(2,1)} copy(bf16[4,8,32,4096]{3,2,1,0:T(8,128)(2,1)} %bitcast.70) | data formatting | bytes 16777216
  357.5 77.8 %reduce-scatter.4.cloned.1.call-done = bf16[8,131072]{1,0:T(8,128)(2,1)} async-done(((bf16[32,131072]{1,0:T(8,128)(2,1)}), bf16[8,131072]{1,0:T(8,128)(2,1)}) %reduce-scatter.4.cloned.1.call-update) | async-done | bytes 2097168
  435.3 8.1 %all-to-all-start.1 = ((bf16[8,32,4096]{2,0,1:T(8,128)(2,1)}), bf16[8,32,4096]{2,0,1:T(8,128)(2,1)}, u32[]{:S(2)}, u32[]{:S(2)}) async-start(bf16[8,32,4096]{2,0,1:T(8,128)(2,1)} %bitcast.72), calls=%async_computation.1 | async-start | bytes 4194304 | tf_op jit(solution)/shard_map/all_to_all | solution.py:164
  444.5 27.1 %all-to-all-done.1 = bf16[8,32,4096]{2,0,1:T(8,128)(2,1)} async-done(((bf16[8,32,4096]{2,0,1:T(8,128)(2,1)}), bf16[8,32,4096]{2,0,1:T(8,128)(2,1)}, u32[]{:S(2)}, u32[]{:S(2)}) %all-to-all-start.1) | async-done | bytes 2097184 | tf_op jit(solution)/shard_map/all_to_all | solution.py:164
  471.6 2.7 copy.67
  474.3 1.2 gather_fusion
  475.5 1.3 reshape.175
  476.9 2.7 reduce_sum.60
  480.2 1.4 multiply_reduce_fusion.1
  481.7 1.8 add_convert_fusion
  (84 shorter events, 8.1 us)
Async XLA Ops:
  6.5 3.1 copy-start
  6.5 73.9 %all-gather.7.cloned.1.call-start = ((), (), s32[]{:S(2)}) async-start(), calls=%async_computation.5 | async-start | bytes 8650752 | tf_op jit(solution)/shard_map/all_gather | solution.py:14
  10.7 118.4 %all-gather.5.cloned.1.call-start = ((), (), s32[]{:S(2)}) async-start(), calls=%async_computation.3 | async-start | bytes 8650752 | tf_op jit(solution)/shard_map/all_gather | solution.py:122
  11.5 167.3 %all-reduce.3.cloned.1.call-start = ((), (), s32[]{:S(2)}) async-start(), calls=%async_computation.4 | async-start | bytes 2097152 | tf_op jit(solution)/shard_map/psum | solution.py:132
  80.3 1.4 copy-start.5
  80.3 1.4 copy-start.7
  80.5 1.7 copy-start.9
  80.5 1.7 copy-start.13
  81.7 2.1 copy-start.6
  81.7 47.5 %copy-start.12 = (f32[1024]{0:T(1024)S(1)}, f32[1024]{0:T(1024)}, u32[]{:S(2)}) copy-start(f32[1024]{0:T(1024)} %param.27) | copy-start | bytes 12292
  92.5 42.6 %copy-start.10 = (s32[128,2]{0,1:T(2,128)S(1)}, s32[128,2]{0,1:T(2,128)}, u32[]{:S(2)}) copy-start(s32[128,2]{0,1:T(2,128)} %param.34) | copy-start | bytes 3076
  92.5 86.3 %copy-start.3 = (bf16[128,4096]{1,0:T(8,128)(2,1)S(1)}, bf16[128,4096]{1,0:T(8,128)(2,1)}, u32[]{:S(2)}) copy-start(bf16[128,4096]{1,0:T(8,128)(2,1)} %param.29) | copy-start | bytes 3145732
  135.0 46.8 %copy-start.8 = (f32[4096]{0:T(1024)S(1)}, f32[4096]{0:T(1024)}, u32[]{:S(2)}) copy-start(f32[4096]{0:T(1024)} %param.30) | copy-start | bytes 49156
  135.1 300.3 %reduce-scatter.4.cloned.1.call-start = ((), (), s32[]{:S(2)}) async-start(), calls=%async_computation.6 | async-start | bytes 10485760
  178.8 3.0 copy-start.4
  301.4 24.4 %slice-start = ((s8[7340032]{0:T(1024)(128)(4,1)}), s8[3145728]{0:T(1024)(128)(4,1)S(1)}, s32[]{:S(2)}) async-start(s8[7340032]{0:T(1024)(128)(4,1)} %bitcast.77), calls=%async_computation.7 | async-start | bytes 6291456
  312.7 13.0 %copy-start.2 = (bf16[32,32,4096]{2,1,0:T(8,128)(2,1)S(1)}, bf16[32,32,4096]{2,1,0:T(8,128)(2,1)}, u32[]{:S(2)}) copy-start(bf16[32,32,4096]{2,1,0:T(8,128)(2,1)} %copy.65) | copy-start | bytes 25165828
  312.7 13.0 %slice-start.1 = ((s8[7340032]{0:T(1024)(128)(4,1)}), s8[4194304]{0:T(1024)(128)(4,1)S(1)}, s32[]{:S(2)}) async-start(s8[7340032]{0:T(1024)(128)(4,1)} %bitcast.77), calls=%async_computation.8 | async-start | bytes 8388608
  312.7 22.2 %slice-start.2 = ((s8[7340032]{0:T(1024)(128)(4,1)}), s8[4194304]{0:T(1024)(128)(4,1)S(1)}, s32[]{:S(2)}) async-start(s8[7340032]{0:T(1024)(128)(4,1)} %bitcast.79), calls=%async_computation.9 | async-start | bytes 8388608
  325.8 9.2 %slice-start.3 = ((s8[7340032]{0:T(1024)(128)(4,1)}), s8[3145728]{0:T(1024)(128)(4,1)S(1)}, s32[]{:S(2)}) async-start(s8[7340032]{0:T(1024)(128)(4,1)} %bitcast.79), calls=%async_computation.10 | async-start | bytes 6291456
  357.5 86.8 %copy-start.11 = (f32[128,2]{0,1:T(2,128)S(1)}, f32[128,2]{0,1:T(2,128)}, u32[]{:S(2)}) copy-start(f32[128,2]{0,1:T(2,128)} %param.35) | copy-start | bytes 3076
  435.3 36.3 %all-to-all-start.1 = ((bf16[8,32,4096]{2,0,1:T(8,128)(2,1)}), bf16[8,32,4096]{2,0,1:T(8,128)(2,1)}, u32[]{:S(2)}, u32[]{:S(2)}) async-start(bf16[8,32,4096]{2,0,1:T(8,128)(2,1)} %bitcast.72), calls=%async_computation.1 | async-start | bytes 4194304 | tf_op jit(solution)/shard_map/all_to_all | solution.py:164
  475.5 8.0 %copy-start.1 = (bf16[128,128]{1,0:T(8,128)(2,1)S(1)}, bf16[128,128]{1,0:T(8,128)(2,1)}, u32[]{:S(2)}) copy-start(bf16[128,128]{1,0:T(8,128)(2,1)} %param.21) | copy-start | bytes 98308
Sparse Core Ops, SparseCore 0:
  10.9 56.8 all-gather.6
  69.9 59.2 all-gather.4
  135.2 43.5 all-reduce.2
  357.7 77.6 reduce-scatter.3
where the time goes:
time: 500 us; the launch traced here: 490 us
  waiting for transfers between devices  185 us (37%)
  blocking collectives  179 us (36%)
  local copies, waits for them, and re-layouts  45.3 us (9%)
  matrix products  44.4 us (9%)
  between operations  14.4 us (3%)
  other arithmetic  13.7 us (3%)
  starting transfers between devices  8.24 us (2%)
    all_to_all x1, blocking collectives, local(): lax.all_to_all(outgoing, 'ctx', split_axis=1, concat_axis=1, tiled=True)  105 us
    unnamed x5, waiting for transfers between devices  78.5 us
    unnamed x1, blocking collectives  65.5 us
    psum x1, waiting for transfers between devices, local(): lax.psum(partial_value.astype(jnp.bfloat16), 'exp').astype(jnp.float32)  42.9 us
    all_gather x1, waiting for transfers between devices, local(): lax.all_gather(out_proj, 'ctx', axis=1, tiled=True)  36.7 us
    all_to_all x1, waiting for transfers between devices, local(): lax.all_to_all(summed, 'ctx', split_axis=1, concat_axis=1, tiled=True)  27.1 us
    unnamed x42, local copies, waits for them, and re-layouts  14.1 us
    dot_general x1, matrix products, local(): up_val = jnp.dot(flattened, up_rows, preferred_element_type=jnp.float32)  13 us
  transfers between devices with their start and end apart: 5, of which 4 were waited for; matrix products, arithmetic and copies ran while one was open for 2% of the time, Pallas kernels for 0%

commit v1 on v0

--- a/solution.py
+++ b/solution.py
@@ -161,7 +161,10 @@
         scatter_dimension=0,
         tiled=True,
     )
-    halves = lax.all_to_all(summed, "ctx", split_axis=1, concat_axis=1, tiled=True)
+    halves = jnp.concatenate(
+        lax.all_to_all(jnp.stack(jnp.split(summed, lax.axis_size("ctx"), axis=1)), "ctx", 0, 0),
+        axis=1,
+    )
     flattened, rank_ids = route_ranks(own_ids, experts)
     base_rows = rank_ids * n_ctx + flattened * PAIR
     fetch_rows = base_rows[:, None] + jnp.arange(PAIR, dtype=jnp.int32)[None, :]

time: 500 us -> 536 us (1.072)
  local copies, waits for them, and re-layouts: 45.3 us -> 80.1 us
    unnamed x42 -> x77, local copies, waits for them, and re-layouts: 14.1 us -> 48.3 us
where the time goes in v1:
time: 536 us; the launch traced here: 525 us
  waiting for transfers between devices  185 us (35%)
  blocking collectives  179 us (33%)
  local copies, waits for them, and re-layouts  80.1 us (15%)
  matrix products  44.4 us (8%)
  between operations  14.4 us (3%)
  other arithmetic  13.7 us (3%)
  starting transfers between devices  8.24 us (2%)
    all_to_all x1, blocking collectives, local(): lax.all_to_all(outgoing, 'ctx', split_axis=1, concat_axis=1, tiled=True)  105 us
    unnamed x5, waiting for transfers between devices  78.5 us
    unnamed x1, blocking collectives  65.5 us
    unnamed x77, local copies, waits for them, and re-layouts  48.3 us
    psum x1, waiting for transfers between devices, local(): lax.psum(partial_value.astype(jnp.bfloat16), 'exp').astype(jnp.float32)  42.9 us
    all_gather x1, waiting for transfers between devices, local(): lax.all_gather(out_proj, 'ctx', axis=1, tiled=True)  36.7 us
    all_to_all x1, waiting for transfers between devices, local(): lax.all_to_all(jnp.stack(jnp.split(summed, lax.axis_size('ctx'), axis=1))...  27.1 us
    dot_general x1, matrix products, local(): up_val = jnp.dot(flattened, up_rows, preferred_element_type=jnp.float32)  13 us
  transfers between devices with their start and end apart: 5, of which 4 were waited for; matrix products, arithmetic and copies ran while one was open for 2% of the time, Pallas kernels for 0%

profile of v1, /device:TPU:1, one launch (start us, length us, event | category | flops | bytes accessed | tf_op | source)
XLA Modules:
  0.0 525.1 jit_solution(3198832525738541760)
XLA Ops:
  13.8 65.5 %all-reduce = bf16[512]{0:T(512)(128)(2,1)S(1)} all-reduce(bf16[512]{0:T(512)(128)(2,1)S(1)} %dynamic-update-slice), channel_id=2, replica_groups=mesh['ctx'=32,'exp'=4] {'ctx'}, use_global_device_ids=true, to_apply=%add | all-reduce | flops 512 | bytes 2048
  84.1 8.4 %psum.14 = f32[128]{0:T(128)S(1)} all-reduce(f32[128]{0:T(128)S(1)} %multiply_reduce_fusion.2), channel_id=1, replica_groups=mesh['ctx'=32,'exp'=4] {'exp'}, use_global_device_ids=true, to_apply=%region_4.5 | all-reduce | flops 128 | bytes 1024 | tf_op jit(solution)/shard_map/psum | solution.py:117
  92.5 36.7 %all-gather.5.cloned.1.call-done = bf16[1024,4096]{1,0:T(8,128)(2,1)} async-done(((bf16[1024,128]{1,0:T(8,128)(2,1)}), bf16[1024,4096]{1,0:T(8,128)(2,1)}) %all-gather.5.cloned.1.call-update) | async-done | bytes 8388624 | tf_op jit(solution)/shard_map/all_gather | solution.py:122
  129.2 5.8 %convolution_convert_fusion.2 = bf16[128,4096]{1,0:T(8,128)(2,1)} fusion(bf16[1024,4096]{1,0:T(8,128)(2,1)} %all-gather.5.cloned.1.call-done, f32[1024]{0:T(1024)S(1)} %copy-done.14, f32[128]{0:T(128)S(1)} %add_rsqrt_fusion.1, f32[128,1024]{1,0:T(8,128)S(1)} %copy.87, bf16[128,1024]{1,0:T(8,128)(2,1)S(1)} %copy-done.8), kind=kOutput, calls=%fused_computation.10 | convolution fusion | flops 1075445760 | bytes 10228224 | tf_op jit(solution)/shard_map/dot_general | solution.py:120
  135.8 42.9 %all-reduce.3.cloned.1.call-done = bf16[128,4096]{1,0:T(8,128)(2,1)} async-done(((bf16[128,4096]{1,0:T(8,128)(2,1)}), bf16[128,4096]{1,0:T(8,128)(2,1)}) %all-reduce.3.cloned.1.call-update) | async-done | bytes 1048592 | tf_op jit(solution)/shard_map/psum | solution.py:132
  178.8 3.0 convert_add_fusion.1
  182.2 3.4 broadcast_in_dim.28
  185.6 2.7 reshape.157
  189.7 2.3 copy.89
  192.1 4.3 broadcast_in_dim.29
  196.3 105.0 %all_to_all.10 = bf16[32,32,4096]{2,0,1:T(8,128)(2,1)} all-to-all(bf16[32,32,4096]{2,0,1:T(8,128)(2,1)} %bitcast.195), channel_id=1, replica_groups=mesh['ctx'=32,'exp'=4] {'ctx'}, dimensions={1} | all-to-all | bytes 16777216 | tf_op jit(solution)/shard_map/all_to_all | solution.py:145
  301.4 11.3 %copy.90 = bf16[32,32,4096]{2,1,0:T(8,128)(2,1)} copy(bf16[32,32,4096]{2,0,1:T(8,128)(2,1)} %all_to_all.10) | data formatting | bytes 16777216 | tf_op jit(solution)/shard_map/all_to_all | solution.py:145
  312.7 13.0 %fusion.1 = f32[1024,896]{1,0:T(8,128)S(1)} fusion(bf16[1024,4096]{1,0:T(8,128)(2,1)} %bitcast.197, bf16[1,4096,896]{2,1,0:T(8,128)(2,1)} %param.32), kind=kOutput, calls=%fused_computation.5 | convolution fusion | flops 7516192768 | bytes 19398656 | tf_op jit(solution)/shard_map/dot_general | solution.py:148
  325.8 9.2 %multiply_convert_fusion = bf16[1024,896]{1,0:T(8,128)(2,1)S(1)} fusion(f32[1024,896]{1,0:T(8,128)S(1)} %fusion.1, bf16[1024,4096]{1,0:T(8,128)(2,1)S(1)} %bitcast.198, bf16[1,4096,896]{2,1,0:T(8,128)(2,1)S(1)} %bitcast.239), kind=kOutput, calls=%fused_computation.11 | convolution fusion | flops 7521697792 | bytes 21233664 | tf_op jit(solution)/shard_map/dot_general | solution.py:147
  335.0 11.2 %convolution_convert_fusion = bf16[1024,4096]{1,0:T(8,128)(2,1)} fusion(bf16[1024,896]{1,0:T(8,128)(2,1)S(1)} %multiply_convert_fusion, bf16[1,896,4096]{2,1,0:T(8,128)(2,1)S(1)} %bitcast.241), kind=kOutput, calls=%fused_computation.3 | convolution fusion | flops 7520387072 | bytes 17563648 | tf_op jit(solution)/shard_map/dot_general | solution.py:152
  346.2 11.3 %copy.99 = bf16[4,8,32,4096]{3,1,2,0:T(8,128)(2,1)} copy(bf16[4,8,32,4096]{3,2,1,0:T(8,128)(2,1)} %bitcast.199) | data formatting | bytes 16777216
  357.5 77.8 %reduce-scatter.4.cloned.1.call-done = bf16[8,131072]{1,0:T(8,128)(2,1)} async-done(((bf16[32,131072]{1,0:T(8,128)(2,1)}), bf16[8,131072]{1,0:T(8,128)(2,1)}) %reduce-scatter.4.cloned.1.call-update) | async-done | bytes 2097168
  435.3 1.6 fusion.65
  436.9 1.5 fusion.64
  438.4 1.5 fusion.63
  441.3 1.5 fusion.61
  442.7 1.5 fusion.60
  444.2 1.5 fusion.59
  448.6 1.5 fusion.56
  450.1 1.5 fusion.55
  454.4 1.5 fusion.52
  455.9 1.5 fusion.51
  468.8 8.1 %all-to-all-start.1 = ((bf16[32,8,1,4096]{3,1,2,0:T(8,128)(2,1)}), bf16[32,8,1,4096]{3,1,2,0:T(8,128)(2,1)S(1)}, u32[]{:S(2)}, u32[]{:S(2)}) async-start(bf16[32,8,1,4096]{3,1,2,0:T(8,128)(2,1)} %fusion.34), calls=%async_computation.1 | async-start | bytes 4194304 | tf_op jit(solution)/shard_map/all_to_all | solution.py:165
  478.0 27.1 %all-to-all-done.1 = bf16[32,8,1,4096]{3,1,2,0:T(8,128)(2,1)S(1)} async-done(((bf16[32,8,1,4096]{3,1,2,0:T(8,128)(2,1)}), bf16[32,8,1,4096]{3,1,2,0:T(8,128)(2,1)S(1)}, u32[]{:S(2)}, u32[]{:S(2)}) %all-to-all-start.1) | async-done | bytes 2097184 | tf_op jit(solution)/shard_map/all_to_all | solution.py:165
  506.4 2.7 copy.92
  511.7 2.7 reduce_sum.60
  516.5 1.8 add_convert_fusion
  (120 shorter events, 40.7 us)
Async XLA Ops:
  6.5 3.1 copy-start
  6.5 73.8 %all-gather.7.cloned.1.call-start = ((), (), s32[]{:S(2)}) async-start(), calls=%async_computation.5 | async-start | bytes 8650752 | tf_op jit(solution)/shard_map/all_gather | solution.py:14
  10.7 118.4 %all-gather.5.cloned.1.call-start = ((), (), s32[]{:S(2)}) async-start(), calls=%async_computation.3 | async-start | bytes 8650752 | tf_op jit(solution)/shard_map/all_gather | solution.py:122
  11.5 167.3 %all-reduce.3.cloned.1.call-start = ((), (), s32[]{:S(2)}) async-start(), calls=%async_computation.4 | async-start | bytes 2097152 | tf_op jit(solution)/shard_map/psum | solution.py:132
  80.4 1.3 copy-start.7
  80.4 1.3 copy-start.9
  80.5 1.7 copy-start.11
  80.5 1.7 copy-start.15
  82.2 1.6 copy-start.8
  82.2 47.0 %copy-start.14 = (f32[1024]{0:T(1024)S(1)}, f32[1024]{0:T(1024)}, u32[]{:S(2)}) copy-start(f32[1024]{0:T(1024)} %param.27) | copy-start | bytes 12292
  92.5 42.6 %copy-start.12 = (s32[128,2]{0,1:T(2,128)S(1)}, s32[128,2]{0,1:T(2,128)}, u32[]{:S(2)}) copy-start(s32[128,2]{0,1:T(2,128)} %param.34) | copy-start | bytes 3076
  135.0 43.7 %copy-start.4 = (bf16[128,4096]{1,0:T(8,128)(2,1)S(1)}, bf16[128,4096]{1,0:T(8,128)(2,1)}, u32[]{:S(2)}) copy-start(bf16[128,4096]{1,0:T(8,128)(2,1)} %param.29) | copy-start | bytes 3145732
  135.1 300.2 %reduce-scatter.4.cloned.1.call-start = ((), (), s32[]{:S(2)}) async-start(), calls=%async_computation.6 | async-start | bytes 10485760
  135.8 45.9 %copy-start.10 = (f32[4096]{0:T(1024)S(1)}, f32[4096]{0:T(1024)}, u32[]{:S(2)}) copy-start(f32[4096]{0:T(1024)} %param.30) | copy-start | bytes 49156
  178.8 3.0 copy-start.5
  301.4 24.4 %slice-start = ((s8[7340032]{0:T(1024)(128)(4,1)}), s8[3145728]{0:T(1024)(128)(4,1)S(1)}, s32[]{:S(2)}) async-start(s8[7340032]{0:T(1024)(128)(4,1)} %bitcast.238), calls=%async_computation.7 | async-start | bytes 6291456
  312.7 13.0 %copy-start.2 = (bf16[32,32,4096]{2,1,0:T(8,128)(2,1)S(1)}, bf16[32,32,4096]{2,1,0:T(8,128)(2,1)}, u32[]{:S(2)}) copy-start(bf16[32,32,4096]{2,1,0:T(8,128)(2,1)} %copy.90) | copy-start | bytes 25165828
  312.7 13.0 %slice-start.1 = ((s8[7340032]{0:T(1024)(128)(4,1)}), s8[4194304]{0:T(1024)(128)(4,1)S(1)}, s32[]{:S(2)}) async-start(s8[7340032]{0:T(1024)(128)(4,1)} %bitcast.238), calls=%async_computation.8 | async-start | bytes 8388608
  312.7 22.2 %slice-start.2 = ((s8[7340032]{0:T(1024)(128)(4,1)}), s8[4194304]{0:T(1024)(128)(4,1)S(1)}, s32[]{:S(2)}) async-start(s8[7340032]{0:T(1024)(128)(4,1)} %bitcast.240), calls=%async_computation.9 | async-start | bytes 8388608
  325.7 9.2 %slice-start.3 = ((s8[7340032]{0:T(1024)(128)(4,1)}), s8[3145728]{0:T(1024)(128)(4,1)S(1)}, s32[]{:S(2)}) async-start(s8[7340032]{0:T(1024)(128)(4,1)} %bitcast.240), calls=%async_computation.10 | async-start | bytes 6291456
  435.3 23.5 %copy-start.6 = (bf16[8,131072]{1,0:T(8,128)(2,1)S(1)}, bf16[8,131072]{1,0:T(8,128)(2,1)}, u32[]{:S(2)}) copy-start(bf16[8,131072]{1,0:T(8,128)(2,1)} %reduce-scatter.4.cloned.1.call-done) | copy-start | bytes 6291460
  468.8 9.0 %copy-start.13 = (f32[128,2]{0,1:T(2,128)S(1)}, f32[128,2]{0,1:T(2,128)}, u32[]{:S(2)}) copy-start(f32[128,2]{0,1:T(2,128)} %param.35) | copy-start | bytes 3076
  468.8 36.3 %all-to-all-start.1 = ((bf16[32,8,1,4096]{3,1,2,0:T(8,128)(2,1)}), bf16[32,8,1,4096]{3,1,2,0:T(8,128)(2,1)S(1)}, u32[]{:S(2)}, u32[]{:S(2)}) async-start(bf16[32,8,1,4096]{3,1,2,0:T(8,128)(2,1)} %fusion.34), calls=%async_computation.1 | async-start | bytes 4194304 | tf_op jit(solution)/shard_map/all_to_all | solution.py:165
  505.1 1.4 copy-start.3
  511.7 6.6 %copy-start.1 = (bf16[128,128]{1,0:T(8,128)(2,1)S(1)}, bf16[128,128]{1,0:T(8,128)(2,1)}, u32[]{:S(2)}) copy-start(bf16[128,128]{1,0:T(8,128)(2,1)} %param.21) | copy-start | bytes 98308
Sparse Core Ops, SparseCore 0:
  10.9 56.8 all-gather.6
  69.9 59.2 all-gather.4
  135.2 43.5 all-reduce.2
  357.6 77.6 reduce-scatter.3
